TPU v7x, 32 devices: a whole 2x2x4 slice. The times are simulated.
32 devices in a mesh: boot: 2 (over x), samp: 16 (over z, y, core).
Axes of the slice: x: 2, y: 2, z: 4, core: 2. Of those that a mesh axis runs over, the one named last changes fastest.
Arguments:
- dosage: bfloat16 [32384, 512], P('samp'), may hold values from 0 to 2, as said below
- residuals: bfloat16 [32384, 1280], P('samp', 'boot'), may hold values from -300 to 300
- maf_bin: int32 [512], replicated, may hold values from 0 to 63
- gene_map: int32 [512], replicated, may hold values from 0 to 31, never falling along the last dimension, each value on 1 to 32 neighbouring positions
- gene_order: int32 [32], replicated, may hold values from 0 to 31, each once
Outputs:
- calibrated: float32 [32, 1280], P('samp', 'boot')
Inputs may be any that keep to these rules, and one draw needn't show every extreme that they name: `dosage`: allele counts 0, 1 or 2. `gene_map`: never falling along the variants; each gene holds 1 to 32 consecutive variants, one gene exactly 32. `gene_order`: each gene once.
All inputs are finite; a program needn't handle non-finite values.
Results may differ from a plain program's by a relative error of at most 0.0003.
Values sent between devices are 32-bit elements; how exact they have to be, the bound alone decides.
A program may use at most 64 MiB of HBM per device.

v0:
```python
import math
import jax
import jax.numpy as jnp
from jax import lax
from jax.sharding import PartitionSpec as P

GENE_DEV = 2
RHOS = 11
MAF_BINS = 64
EPSILON = 1e-05


def variant_weights(maf_bin):
    levels = jnp.arange(MAF_BINS, dtype=jnp.float32)
    weight_table = (1.0 - 0.05 * (levels + 0.5) / MAF_BINS) ** 24
    matches = maf_bin[:, None] == jnp.arange(MAF_BINS, dtype=jnp.int32)[None, :]
    return jnp.sum(
        jnp.where(matches, weight_table[None, :], jnp.zeros_like(weight_table)[None, :]), axis=1
    )


def sample_product(dose_part, residuals):
    return lax.dot_general(
        dose_part, residuals, (((0,), (0,)), ((), ())), preferred_element_type=jnp.float32
    )


def shards(dosage, residuals, maf_bin, gene_map, gene_order):
    sample_total = dosage.shape[0] * lax.axis_size("samp")
    scaling = variant_weights(maf_bin) / math.sqrt(sample_total)
    my_index = lax.axis_index("samp")
    partial_value = sample_product(dosage, residuals) * scaling[:, None]
    scores = lax.psum(partial_value, "samp")
    owned_genes = lax.dynamic_slice_in_dim(gene_order, my_index * GENE_DEV, GENE_DEV)
    member = (owned_genes[:, None] == gene_map[None, :]).astype(jnp.float32)
    stacked = jnp.concatenate([scores, scores * scores], axis=1)
    gene_sums = jnp.dot(
        member, stacked, precision=lax.Precision.HIGHEST, preferred_element_type=jnp.float32
    )
    boot_local = residuals.shape[1]
    burden = gene_sums[:, :boot_local]
    skat = gene_sums[:, boot_local:]
    rho_grid = jnp.arange(RHOS, dtype=jnp.float32) / (RHOS - 1)
    mixtures = (1.0 - rho_grid)[None, :, None] * skat[:, None, :] + rho_grid[None, :, None] * (
        burden * burden
    )[:, None, :]
    boot_total = boot_local * lax.axis_size("boot")
    first_sum, square_sum = lax.psum(
        (jnp.sum(mixtures, axis=2), jnp.sum(mixtures * mixtures, axis=2)), "boot"
    )
    center = first_sum / boot_total
    spread = square_sum / boot_total - center * center
    deviation = mixtures - center[:, :, None]
    zscore = deviation / jnp.sqrt(spread[:, :, None] + EPSILON)
    return jnp.max(zscore, axis=1)


def solution(mesh):
    placed = (P("samp", None), P("samp", "boot"), P(), P(), P())
    return jax.shard_map(
        shards, mesh=mesh, in_specs=placed, out_specs=P("samp", "boot"), check_vma=False
    )
```

profile of v0, /device:TPU:0, one launch (start us, length us, event | category | flops | bytes accessed | tf_op | source)
XLA Modules:
  0.0 128.8 jit_solution(401770869329293279)
XLA Ops:
  6.5 0.0 copy-start
  6.5 0.0 all-reduce.3.cloned.1.call-start
  6.6 0.9 select_reduce_fusion
  7.5 0.8 copy-done
  8.3 0.0 copy-start.3
  8.3 4.5 %convolution_multiply_fusion = f32[512,640]{1,0:T(8,128)} fusion(bf16[2024,512]{1,0:T(8,128)(2,1)} %param.5, bf16[2024,640]{1,0:T(8,128)(2,1)S(1)} %copy-done, f32[512]{0:T(512)S(1)} %broadcast_multiply_fusion.1), kind=kOutput, calls=%fused_computation.4 | convolution fusion | flops 1326776320 | bytes 5976064 | tf_op jit(solution)/shard_map/dot_general | solution.py:23
  12.8 0.0 all-reduce.3.cloned.1.call-update
  12.8 0.0 copy-start.2
  12.8 0.0 copy-done.3
  12.9 0.1 dynamic_slice.3
  12.9 96.9 %all-reduce.3.cloned.1.call-done = f32[512,640]{1,0:T(8,128)} async-done(((f32[512,640]{1,0:T(8,128)}), f32[512,640]{1,0:T(8,128)}) %all-reduce.3.cloned.1.call-update) | async-done | bytes 1310736 | tf_op jit(solution)/shard_map/psum | solution.py:33
  109.8 0.0 copy-start.1
  109.8 1.9 %mul.96 = f32[512,640]{1,0:T(8,128)S(1)} multiply(f32[512,640]{1,0:T(8,128)} %all-reduce.3.cloned.1.call-done, f32[512,640]{1,0:T(8,128)} %all-reduce.3.cloned.1.call-done) | non-fusion elementwise | flops 327680 | bytes 3932160 | tf_op jit(solution)/shard_map/mul | solution.py:36
  111.7 0.0 copy-done.2
  111.8 0.1 copy-done.1
  111.9 1.0 fusion
  112.9 0.2 fusion.5
  113.1 8.1 %all-reduce = (f32[2,11]{0,1:T(8,128)S(1)}, f32[2,11]{0,1:T(8,128)S(1)}) all-reduce(f32[2,11]{0,1:T(8,128)S(1)} %get-tuple-element.6, f32[2,11]{0,1:T(8,128)S(1)} %get-tuple-element.5), channel_id=1, replica_groups=mesh['boot'=2,'samp'=16] {'boot'}, use_global_device_ids=true, to_apply=%region_5.6 | all-reduce | flops 44 | bytes 352 | tf_op jit(solution)/shard_map/psum | solution.py:48
  121.2 0.7 fusion.4
  (5 shorter events, 0.1 us)
Async XLA Ops:
  6.5 1.7 %copy-start = (bf16[2024,640]{1,0:T(8,128)(2,1)S(1)}, bf16[2024,640]{1,0:T(8,128)(2,1)}, u32[]{:S(2)}) copy-start(bf16[2024,640]{1,0:T(8,128)(2,1)} %param.6) | copy-start | bytes 7772164
  6.5 103.3 %all-reduce.3.cloned.1.call-start = ((), (), s32[]{:S(2)}) async-start(), calls=%async_computation | async-start | bytes 2621440 | tf_op jit(solution)/shard_map/psum | solution.py:33
  8.3 4.6 %copy-start.3 = (s32[32]{0:T(128)S(1)}, s32[32]{0:T(128)}, u32[]{:S(2)}) copy-start(s32[32]{0:T(128)} %param.9) | copy-start | bytes 388
  12.8 98.9 %copy-start.2 = (s32[512]{0:T(512)S(1)}, s32[512]{0:T(512)}, u32[]{:S(2)}) copy-start(s32[512]{0:T(512)} %param.8) | copy-start | bytes 6148
  109.8 2.1 %copy-start.1 = (f32[512,640]{1,0:T(8,128)S(1)}, f32[512,640]{1,0:T(8,128)}, u32[]{:S(2)}) copy-start(f32[512,640]{1,0:T(8,128)} %all-reduce.3.cloned.1.call-done) | copy-start | bytes 3932164
Sparse Core Ops, SparseCore 0:
  12.9 96.7 all-reduce.2
where the time goes:
time: 129 us
  waiting for transfers between devices  96.9 us (75%)
  between operations  13.4 us (10%)
  blocking collectives  8.14 us (6%)
  matrix products  5.49 us (4%)
  other arithmetic  3.86 us (3%)
    psum x1, waiting for transfers between devices, shards(): scores = lax.psum(partial_value, 'samp')  96.9 us
    psum x1, blocking collectives, shards(): lax.psum((jnp.sum(mixtures, axis=2), jnp.sum(mixtures * mixtures, axis=2)...  8.14 us
    dot_general x1, matrix products, sample_product(): lax.dot_general(dose_part, residuals, (((0,), (0,)), ((), ())), preferred...  4.52 us
  transfers between devices with their start and end apart: 1, of which 1 were waited for; matrix products, arithmetic and copies ran while one was open for 0% of the time, Pallas kernels for 0%

commit v1 on v0

--- a/solution.py
+++ b/solution.py
@@ -30,7 +30,9 @@
     scaling = variant_weights(maf_bin) / math.sqrt(sample_total)
     my_index = lax.axis_index("samp")
     partial_value = sample_product(dosage, residuals) * scaling[:, None]
-    scores = lax.psum(partial_value, "samp")
+    scores = partial_value
+    for hop in (1, 2, 4, 8):
+        scores = scores + lax.ppermute(scores, "samp", [(dev, dev ^ hop) for dev in range(16)])
     owned_genes = lax.dynamic_slice_in_dim(gene_order, my_index * GENE_DEV, GENE_DEV)
     member = (owned_genes[:, None] == gene_map[None, :]).astype(jnp.float32)
     stacked = jnp.concatenate([scores, scores * scores], axis=1)

time: 129 us -> 143 us (1.11)
  waiting for transfers between devices: 96.9 us -> 116 us
  between operations: 13.4 us -> 0.05 us
  starting transfers between devices: 0.01 us -> 7.89 us
    ppermute x0 -> x4, waiting for transfers between devices: none -> 116 us  [shards(): lax.ppermute(scores, 'samp', [(dev, dev ^ hop) for dev in range(16)])]
    psum x1 -> x0, waiting for transfers between devices: 96.9 us -> none  [shards(): scores = lax.psum(partial_value, 'samp')]
    ppermute x0 -> x4, starting transfers between devices: none -> 7.89 us  [shards(): lax.ppermute(scores, 'samp', [(dev, dev ^ hop) for dev in range(16)])]
    add x0 -> x3, other arithmetic: none -> 1.46 us  [shards(): scores + lax.ppermute(scores, 'samp', [(dev, dev ^ hop) for dev in range(...]
  transfers between devices with their start and end apart: 1 -> 4, of which waited for: 1 -> 4; matrix products, arithmetic and copies ran while one was open for 0% -> 0% of each run, Pallas kernels for 0% -> 0%
where the time goes in v1:
time: 143 us
  waiting for transfers between devices  116 us (81%)
  starting transfers between devices  7.89 us (6%)
  blocking collectives  7.83 us (5%)
  other arithmetic  5.25 us (4%)
  matrix products  4.39 us (3%)
    ppermute x4, waiting for transfers between devices, shards(): lax.ppermute(scores, 'samp', [(dev, dev ^ hop) for dev in range(16)])  116 us
    ppermute x4, starting transfers between devices, shards(): lax.ppermute(scores, 'samp', [(dev, dev ^ hop) for dev in range(16)])  7.89 us
    psum x1, blocking collectives, shards(): lax.psum((jnp.sum(mixtures, axis=2), jnp.sum(mixtures * mixtures, axis=2)...  7.83 us
    dot_general x1, matrix products, sample_product(): lax.dot_general(dose_part, residuals, (((0,), (0,)), ((), ())), preferred...  3.43 us
  transfers between devices with their start and end apart: 4, of which 4 were waited for; matrix products, arithmetic and copies ran while one was open for 0% of the time, Pallas kernels for 0%

profile of v1, /device:TPU:0, one launch (start us, length us, event | category | flops | bytes accessed | tf_op | source)
XLA Modules:
  0.0 142.6 jit_solution(15410449317402304512)
XLA Ops:
  0.0 0.0 copy-start
  0.0 0.9 select_reduce_fusion
  1.0 0.8 copy-done
  1.7 3.4 %convolution_multiply_fusion = f32[512,640]{1,0:T(8,128)S(1)} fusion(bf16[2024,512]{1,0:T(8,128)(2,1)} %param.5, bf16[2024,640]{1,0:T(8,128)(2,1)S(1)} %copy-done, f32[512]{0:T(512)S(1)} %broadcast_multiply_fusion.1), kind=kOutput, calls=%fused_computation.4 | convolution fusion | flops 1326776320 | bytes 5976064 | tf_op jit(solution)/shard_map/dot_general | solution.py:23
  5.2 0.6 collective-permute-start
  5.7 2.7 %collective-permute-done = f32[512,640]{1,0:T(8,128)S(1)} collective-permute-done((f32[512,640]{1,0:T(8,128)S(1)}, f32[512,640]{1,0:T(8,128)S(1)}, u32[]{:S(2)}, u32[]{:S(2)}) %collective-permute-start) | collective-permute-done | bytes 1310752 | tf_op jit(solution)/shard_map/ppermute | solution.py:35
  8.4 0.1 add.39
  8.5 2.9 %collective-permute-start.1 = (f32[512,640]{1,0:T(8,128)S(1)}, f32[512,640]{1,0:T(8,128)S(1)}, u32[]{:S(2)}, u32[]{:S(2)}) collective-permute-start(f32[512,640]{1,0:T(8,128)S(1)} %add.39), channel_id=1, source_target_pairs={{0,2},{1,3},{2,0},{3,1},{4,6},{5,7},{6,4},{7,5},{8,10},{9,11},{10,... | collective-permute-start | bytes 3932168 | tf_op jit(solution)/shard_map/ppermute | solution.py:35
  11.5 29.1 %collective-permute-done.1 = f32[512,640]{1,0:T(8,128)S(1)} collective-permute-done((f32[512,640]{1,0:T(8,128)S(1)}, f32[512,640]{1,0:T(8,128)S(1)}, u32[]{:S(2)}, u32[]{:S(2)}) %collective-permute-start.1) | collective-permute-done | bytes 1310752 | tf_op jit(solution)/shard_map/ppermute | solution.py:35
  40.6 0.1 add.40
  40.7 0.0 copy-start.2
  40.7 1.9 %collective-permute-start.2 = (f32[512,640]{1,0:T(8,128)S(1)}, f32[512,640]{1,0:T(8,128)S(1)}, u32[]{:S(2)}, u32[]{:S(2)}) collective-permute-start(f32[512,640]{1,0:T(8,128)S(1)} %add.40), channel_id=1, source_target_pairs={{0,4},{1,5},{2,6},{3,7},{4,0},{5,1},{6,2},{7,3},{8,12},{9,13},{10,... | collective-permute-start | bytes 3932168 | tf_op jit(solution)/shard_map/ppermute | solution.py:35
  42.6 28.4 %collective-permute-done.2 = f32[512,640]{1,0:T(8,128)S(1)} collective-permute-done((f32[512,640]{1,0:T(8,128)S(1)}, f32[512,640]{1,0:T(8,128)S(1)}, u32[]{:S(2)}, u32[]{:S(2)}) %collective-permute-start.2) | collective-permute-done | bytes 1310752 | tf_op jit(solution)/shard_map/ppermute | solution.py:35
  71.0 1.2 add.41
  72.2 2.5 %collective-permute-start.3 = (f32[512,640]{1,0:T(8,128)}, f32[512,640]{1,0:T(8,128)}, u32[]{:S(2)}, u32[]{:S(2)}) collective-permute-start(f32[512,640]{1,0:T(8,128)} %add.41), channel_id=1, source_target_pairs={{0,8},{1,9},{2,10},{3,11},{4,12},{5,13},{6,14},{7,15},{8,0},{9,1},... | collective-permute-start | bytes 3932168 | tf_op jit(solution)/shard_map/ppermute | solution.py:35
  74.7 0.0 copy-done.2
  74.7 0.1 dynamic_slice.3
  74.8 0.0 copy-start.1
  74.8 56.1 %collective-permute-done.3 = f32[512,640]{1,0:T(8,128)} collective-permute-done((f32[512,640]{1,0:T(8,128)}, f32[512,640]{1,0:T(8,128)}, u32[]{:S(2)}, u32[]{:S(2)}) %collective-permute-start.3) | collective-permute-done | bytes 1310752 | tf_op jit(solution)/shard_map/ppermute | solution.py:35
  130.9 1.9 %fusion.10 = (f32[512,640]{1,0:T(8,128)S(1)}, f32[512,640]{1,0:T(8,128)S(1)}) fusion(f32[512,640]{1,0:T(8,128)} %add.41, f32[512,640]{1,0:T(8,128)} %collective-permute-done.3), kind=kLoop, calls=%fused_computation.23 | loop fusion | flops 655360 | bytes 5242880 | tf_op jit(solution)/shard_map/mul | solution.py:38
  132.8 0.0 copy-done.1
  132.8 1.0 fusion
  133.8 0.2 fusion.5
  134.0 7.8 %all-reduce = (f32[2,11]{0,1:T(8,128)S(1)}, f32[2,11]{0,1:T(8,128)S(1)}) all-reduce(f32[2,11]{0,1:T(8,128)S(1)} %get-tuple-element.6, f32[2,11]{0,1:T(8,128)S(1)} %get-tuple-element.5), channel_id=1, replica_groups=mesh['boot'=2,'samp'=16] {'boot'}, use_global_device_ids=true, to_apply=%region_4.5 | all-reduce | flops 44 | bytes 352 | tf_op jit(solution)/shard_map/psum | solution.py:50
  141.8 0.7 fusion.4
  (5 shorter events, 0.1 us)
Async XLA Ops:
  0.0 1.7 %copy-start = (bf16[2024,640]{1,0:T(8,128)(2,1)S(1)}, bf16[2024,640]{1,0:T(8,128)(2,1)}, u32[]{:S(2)}) copy-start(bf16[2024,640]{1,0:T(8,128)(2,1)} %param.6) | copy-start | bytes 7772164
  5.2 3.2 %collective-permute-start = (f32[512,640]{1,0:T(8,128)S(1)}, f32[512,640]{1,0:T(8,128)S(1)}, u32[]{:S(2)}, u32[]{:S(2)}) collective-permute-start(f32[512,640]{1,0:T(8,128)S(1)} %convolution_multiply_fusion), channel_id=1, source_target_pairs={{0,1},{1,0},{2,3},{3,2},{4,5},{5,4},{6,7},{7,6},{8,9},{9,8},{10,11... | collective-permute-start | bytes 3932168 | tf_op jit(solution)/shard_map/ppermute | solution.py:35
  8.5 32.0 %collective-permute-start.1 = (f32[512,640]{1,0:T(8,128)S(1)}, f32[512,640]{1,0:T(8,128)S(1)}, u32[]{:S(2)}, u32[]{:S(2)}) collective-permute-start(f32[512,640]{1,0:T(8,128)S(1)} %add.39), channel_id=1, source_target_pairs={{0,2},{1,3},{2,0},{3,1},{4,6},{5,7},{6,4},{7,5},{8,10},{9,11},{10,... | collective-permute-start | bytes 3932168 | tf_op jit(solution)/shard_map/ppermute | solution.py:35
  40.7 34.0 %copy-start.2 = (s32[32]{0:T(128)S(1)}, s32[32]{0:T(128)}, u32[]{:S(2)}) copy-start(s32[32]{0:T(128)} %param.9) | copy-start | bytes 388
  40.7 30.3 %collective-permute-start.2 = (f32[512,640]{1,0:T(8,128)S(1)}, f32[512,640]{1,0:T(8,128)S(1)}, u32[]{:S(2)}, u32[]{:S(2)}) collective-permute-start(f32[512,640]{1,0:T(8,128)S(1)} %add.40), channel_id=1, source_target_pairs={{0,4},{1,5},{2,6},{3,7},{4,0},{5,1},{6,2},{7,3},{8,12},{9,13},{10,... | collective-permute-start | bytes 3932168 | tf_op jit(solution)/shard_map/ppermute | solution.py:35
  72.2 58.7 %collective-permute-start.3 = (f32[512,640]{1,0:T(8,128)}, f32[512,640]{1,0:T(8,128)}, u32[]{:S(2)}, u32[]{:S(2)}) collective-permute-start(f32[512,640]{1,0:T(8,128)} %add.41), channel_id=1, source_target_pairs={{0,8},{1,9},{2,10},{3,11},{4,12},{5,13},{6,14},{7,15},{8,0},{9,1},... | collective-permute-start | bytes 3932168 | tf_op jit(solution)/shard_map/ppermute | solution.py:35
  74.8 58.0 %copy-start.1 = (s32[512]{0:T(512)S(1)}, s32[512]{0:T(512)}, u32[]{:S(2)}) copy-start(s32[512]{0:T(512)} %param.8) | copy-start | bytes 6148
